TPU v7x, 32 devices: a whole 2x2x4 slice. The times are simulated.
32 devices in a mesh: ax: 4 (over y, x), az: 8 (over z, core).
Axes of the slice: x: 2, y: 2, z: 4, core: 2. Of those that a mesh axis runs over, the one named last changes fastest.
Arguments:
- velocity: float32 [3, 64, 512, 512], P(None, 'ax', 'az'), may hold values from -6 to 6
- viscosity: float32 [64, 512, 512], P('ax', 'az'), may hold values from 0.5 to 4
- force: float32 [3, 8192, 512], P(None, ('ax', 'az')), may hold values from -6 to 6
- area: float32 [8192], P(('ax', 'az')), may hold values from 0.5 to 2
- adjacency: int32 [8192, 4], P(('ax', 'az')), may hold values from 0 to 8191, as said below
- crossing: int32 [8192, 1], P(('ax', 'az')), may hold values from 0 to 31; in each aligned block of 256 rows (0 to 255, 256 to 511, ...) at most 16 rows name the same one
- cell: int32 [8192], P(('ax', 'az')), may hold values from 0 to 1023
Outputs:
- updated: float32 [3, 64, 512, 512], P(None, 'ax', 'az')
Inputs may be any that keep to these rules, and one draw needn't show every extreme that they name: adjacency[p, k] differs from p by at most 32; the first neighbour of a panel lies exactly 32 away unless the surface ends there. `crossing`: among the panels of one device no brick is crossed by more than 16 panels, a bound that some block reaches.
All inputs are finite; a program needn't handle non-finite values.
Results may differ from a plain program's by a relative error of at most 0.000062.
Values sent between devices are 32-bit elements; how exact they have to be, the bound alone decides.
A program may use at most 128 MiB of HBM per device.

v0:
```python
import jax
import jax.numpy as jnp
from jax import lax
from jax.sharding import PartitionSpec as P

HALO = 32


step_size = 0.1
coupling = 0.2


def padded(x, sides, width, wrap):
    for axis, dim in sides:
        peers, length = (lax.axis_size(axis), x.shape[dim])
        up = [(i, (i + 1) % peers) for i in range(peers if wrap else peers - 1)]
        down = [(j, i) for i, j in up]
        last = lax.slice_in_dim(x, length - width, length, axis=dim)
        initial = lax.slice_in_dim(x, 0, width, axis=dim)
        before = lax.ppermute(last, axis, up)
        after = lax.ppermute(initial, axis, down)
        x = jnp.concatenate([before, x, after], axis=dim)
    return x


def face_term(mu, mu_other, field, field_other):
    return 0.5 * (mu + mu_other)[None] * (field_other - field)


def on_device(velocity, viscosity, force, area, adjacency, crossing, cell):
    pan_dev = force.shape[1]
    radial = force.shape[2]
    bricks = lax.axis_size(("ax", "az"))
    capacity = max(2, 2 * pan_dev // bricks)
    extended = padded(force, ((("ax", "az"), 1),), HALO, False)
    base = lax.axis_index(("ax", "az")) * pan_dev - HALO
    local_adj = adjacency - base
    neighbours = jnp.take(extended, local_adj, axis=1)
    jump = area[None, :, None] * (
        force + coupling * jnp.sum(neighbours - force[:, :, None, :], axis=2)
    )
    tiles = jnp.transpose(jump, (1, 0, 2)).reshape(pan_dev, 3 * radial)
    dest = crossing[:, 0]
    same = dest[:, None] == dest[None, :]
    rows_iota = lax.broadcasted_iota(jnp.int32, (pan_dev, pan_dev), 0)
    cols_iota = lax.broadcasted_iota(jnp.int32, (pan_dev, pan_dev), 1)
    slot = jnp.sum((same & (cols_iota < rows_iota)).astype(jnp.int32), axis=1)
    target = dest * capacity + slot
    slot_ids = jnp.arange(bricks * capacity, dtype=jnp.int32)
    hits = target[:, None] == slot_ids[None, :]
    placing = hits.astype(jnp.float32)
    send_tiles = jnp.dot(placing.T, tiles, precision=lax.Precision.HIGHEST)
    send_cells = jnp.sum(hits.astype(jnp.int32) * (cell + 1)[:, None], axis=0) - 1
    got_tiles, got_cells = (
        lax.all_to_all(
            send_tiles.reshape(bricks, capacity, 3 * radial),
            ("ax", "az"),
            split_axis=0,
            concat_axis=0,
            tiled=True,
        ),
        lax.all_to_all(
            send_cells.reshape(bricks, capacity),
            ("ax", "az"),
            split_axis=0,
            concat_axis=0,
            tiled=True,
        ),
    )
    got_tiles = got_tiles.reshape(bricks * capacity, 3 * radial)
    got_cells = got_cells.reshape(bricks * capacity)
    n_axial = velocity.shape[1]
    n_azim = velocity.shape[2]
    columns = jnp.arange(n_axial * n_azim, dtype=jnp.int32)
    landing = (got_cells[None, :] == columns[:, None]).astype(jnp.float32)
    deposit = jnp.dot(landing, got_tiles, precision=lax.Precision.HIGHEST)
    deposit = jnp.transpose(deposit.reshape(n_axial, n_azim, 3, radial), (2, 0, 1, 3))
    stacked = jnp.concatenate([velocity, viscosity[None]], axis=0)
    axial_ext = padded(stacked, (("ax", 1),), 1, False)
    azim_ext = padded(stacked, (("az", 2),), 1, True)
    total = face_term(viscosity, axial_ext[3, 2:], velocity, axial_ext[:3, 2:])
    total = total + face_term(viscosity, axial_ext[3, :-2], velocity, axial_ext[:3, :-2])
    total = total + face_term(viscosity, azim_ext[3, :, 2:], velocity, azim_ext[:3, :, 2:])
    total = total + face_term(viscosity, azim_ext[3, :, :-2], velocity, azim_ext[:3, :, :-2])
    fpad = jnp.pad(velocity, ((0, 0), (0, 0), (0, 0), (1, 1)))
    mpad = jnp.pad(viscosity, ((0, 0), (0, 0), (1, 1)))
    total = total + face_term(viscosity, mpad[:, :, 2:], velocity, fpad[:, :, :, 2:])
    total = total + face_term(viscosity, mpad[:, :, :-2], velocity, fpad[:, :, :, :-2])
    return velocity + step_size * total + deposit


def solution(mesh):
    in_specs = (
        P(None, "ax", "az", None),
        P("ax", "az", None),
        P(None, ("ax", "az"), None),
        P(("ax", "az")),
        P(("ax", "az"), None),
        P(("ax", "az"), None),
        P(("ax", "az")),
    )
    out_specs = P(None, "ax", "az", None)
    return jax.shard_map(
        on_device, mesh=mesh, in_specs=in_specs, out_specs=out_specs, check_vma=False
    )
```

profile of v0, /device:TPU:9, one launch (start us, length us, event | category | flops | bytes accessed | tf_op | source)
XLA Modules:
  0.0 177.6 jit_solution(3597815927935226398)
XLA Ops:
  0.0 2.5 %copy.87 = f32[3,256,512]{2,0,1:T(4,128)S(1)} copy(f32[3,256,512]{2,1,0:T(8,128)} %param.9) | data formatting | bytes 3145728 | tf_op args[2]
  2.5 1.3 copy-done.2
  4.0 3.8 %collective-permute-start.4 = (f32[3,32,512]{2,0,1:T(4,128)S(1)}, f32[3,32,512]{2,0,1:T(4,128)S(1)}, u32[]{:S(2)}, u32[]{:S(2)}) collective-permute-start(f32[3,32,512]{2,0,1:T(4,128)S(1)} %get-tuple-element.17), channel_id=1, source_target_pairs={{0,1},{1,2},{2,3},{3,4},{4,5},{5,6},{6,7},{7,8},{8,9},{9,10},{10,1... | collective-permute-start | bytes 589832 | tf_op jit(solution)/shard_map/ppermute | solution.py:20
  7.7 1.9 %collective-permute-start.5 = (f32[3,32,512]{2,0,1:T(4,128)S(1)}, f32[3,32,512]{2,0,1:T(4,128)S(1)}, u32[]{:S(2)}, u32[]{:S(2)}) collective-permute-start(f32[3,32,512]{2,0,1:T(4,128)S(1)} %get-tuple-element.18), channel_id=1, source_target_pairs={{1,0},{2,1},{3,2},{4,3},{5,4},{6,5},{7,6},{8,7},{9,8},{10,9},{11,1... | collective-permute-start | bytes 589832 | tf_op jit(solution)/shard_map/ppermute | solution.py:21
  9.7 0.2 convert_reduce_fusion
  9.9 0.1 select_reduce_fusion
  10.0 0.7 sub.48
  10.7 6.2 %all-to-all-start = ((s32[32,1,16]{2,1,0:T(1,128)}), s32[32,1,16]{2,1,0:T(1,128)S(1)}, u32[]{:S(2)}, u32[]{:S(2)}) async-start(s32[32,1,16]{2,1,0:T(1,128)} %bitcast.8), calls=%async_computation | async-start | bytes 32768 | tf_op jit(solution)/shard_map/all_to_all | solution.py:62
  17.2 0.2 copy.86
  17.5 2.2 %pad_maximum_fusion.8 = f32[3,320,512]{2,0,1:T(4,128)S(1)} fusion(f32[3,32,512]{2,0,1:T(4,128)S(1)} %collective-permute-done.5, f32[3,256,512]{2,0,1:T(4,128)} %copy-done.2, f32[3,32,512]{2,0,1:T(4,128)S(1)} %collective-permute-done.4), kind=kLoop, calls=%fused_computation.35 | loop fusion | flops 983040 | bytes 3932160 | tf_op jit(solution)/shard_map/concatenate | solution.py:22
  19.6 13.3 %gather_fusion = f32[1024,3,512]{2,1,0:T(4,128)} fusion(f32[3,320,512]{2,0,1:T(4,128)S(1)} %pad_maximum_fusion.8, s32[1024]{0:T(1024)S(1)} %broadcast_clamp_fusion), kind=kCustom, calls=%fused_computation | custom fusion | bytes 12587008 | tf_op jit(solution)/shard_map/jit(_take)/gather | solution.py:38
  32.9 7.3 %fusion = f32[3,256,512]{2,0,1:T(4,128)S(1)} fusion(f32[256,4,3,512]{3,2,1,0:T(4,128)} %bitcast.62, f32[3,256,512]{2,0,1:T(4,128)} %copy-done.2, pred[256,4]{1,0:T(8,128)(4,1)S(1)} %copy.86), kind=kLoop, calls=%fused_computation.2 | loop fusion | flops 4325376 | bytes 9438208 | tf_op jit(solution)/shard_map/reduce_sum | solution.py:40
  40.3 0.6 fusion.36
  40.9 0.5 copy.93
  41.4 3.2 %fusion.39 = f32[32,16,1536]{2,1,0:T(8,128)} fusion(f32[256,1536,1]{0,1,2:T(8,128)S(1)} %bitcast.64, s32[32,16]{1,0:T(8,128)S(1)} %multiply_add_fusion, s32[256]{0:T(256)S(1)} %bitcast.67), kind=kOutput, calls=%fused_computation.64 | convolution fusion | flops 2416050176 | bytes 4721664 | tf_op jit(solution)/shard_map/dot_general | solution.py:52
  44.5 6.0 %all-to-all-start.1 = ((f32[32,16,1536]{2,1,0:T(8,128)}), f32[32,16,1536]{2,1,0:T(8,128)}, u32[]{:S(2)}, u32[]{:S(2)}) async-start(f32[32,16,1536]{2,1,0:T(8,128)} %fusion.39), calls=%async_computation.1 | async-start | bytes 6291456 | tf_op jit(solution)/shard_map/all_to_all | solution.py:55
  50.5 2.4 %pad_maximum_fusion.10 = (f32[4,1,64,512]{3,2,1,0:T(8,128)}, f32[4,1,64,512]{3,2,1,0:T(8,128)}) fusion(f32[1,16,64,512]{3,2,1,0:T(8,128)} %bitcast.58, f32[3,16,64,512]{3,2,1,0:T(8,128)} %param.7), kind=kLoop, calls=%fused_computation.61 | loop fusion | flops 262144 | bytes 9437184 | tf_op jit(solution)/shard_map/slice | solution.py:19
  53.0 1.4 collective-permute-start
  54.4 4.0 %collective-permute-start.1 = (f32[4,1,64,512]{3,2,1,0:T(8,128)}, f32[4,1,64,512]{3,2,1,0:T(8,128)S(1)}, u32[]{:S(2)}, u32[]{:S(2)}) collective-permute-start(f32[4,1,64,512]{3,2,1,0:T(8,128)} %get-tuple-element.14), channel_id=1, source_target_pairs={{0,8},{8,16},{16,24},{1,9},{9,17},{17,25},{2,10},{10,18},{18,26},{... | collective-permute-start | bytes 1572872 | tf_op jit(solution)/shard_map/ppermute | solution.py:20
  58.5 0.9 pad_maximum_fusion.12
  59.4 1.0 collective-permute-start.2
  60.3 1.1 collective-permute-start.3
  61.4 3.6 %copy.84 = f32[3,16,64,512]{3,2,0,1:T(8,128)} copy(f32[3,16,64,512]{3,2,1,0:T(8,128)S(1)} %bitcast.57) | data formatting | bytes 12582912 | tf_op args[0]
  65.0 0.6 multiply_add_fusion.1
  65.6 0.5 broadcast.103
  66.1 0.6 reduce.3
  66.8 56.7 %collective-permute-done.2 = f32[4,16,1,512]{3,2,1,0:T(1,128)S(1)} collective-permute-done((f32[4,16,1,512]{3,2,1,0:T(1,128)}, f32[4,16,1,512]{3,2,1,0:T(1,128)S(1)}, u32[]{:S(2)}, u32[]{:S(2)}) %collective-permute-start.2) | collective-permute-done | bytes 131104 | tf_op jit(solution)/shard_map/ppermute | solution.py:21
  123.5 9.3 %fusion.25 = (f32[16,64,512]{2,1,0:T(8,128)}, f32[16,64,512]{2,1,0:T(8,128)S(1)}, f32[16,64,512]{2,1,0:T(8,128)S(1)}, f32[16,64,512]{2,1,0:T(8,128)S(1)}, f32[16,64,512]{2,1,0:T(8,128)}, /*index=5*/f32[16,64,512]{2,1,0:T(8,128)}) fusion(f32[16,64,512]{2,1,0:T(8,128)} %param.8, f32[4,16,1,512]{3,2,1,0:T(1,128)S(1)} %collective-permute-done.3, ...), kind=kLoop, calls=%fused_computation.42 | loop fusion | flops 10485760 | bytes 24379392 | tf_op jit(solution)/shard_map/mul | solution.py:27
  132.7 17.2 %fusion.12 = (f32[3,16,64,512]{3,2,1,0:T(8,128)}, f32[3,16,64,512]{3,2,1,0:T(8,128)}) fusion(f32[3,16,64,512]{3,2,1,0:T(8,128)} %param.7, f32[4,16,1,512]{3,2,1,0:T(1,128)S(1)} %collective-permute-done.2, f32[1,16,64,512]{3,2,1,0:T(8,128)S(1)} %bitcast.61, f32[4,1,64,512]{3,2,1,0:T(8,128)S(1)} %collective-permute-done.1, ...), kind=kLoop, calls=%fused_computation.19 | loop fusion | flops 25165824 | bytes 28573696 | tf_op jit(solution)/shard_map/add | solution.py:83
  149.9 2.4 %copy.95 = f32[1536,512]{1,0:T(8,128)S(1)} copy(f32[1536,512]{0,1:T(8,128)} %bitcast.17) | data formatting | bytes 6291456 | tf_op jit(solution)/shard_map/dot_general | solution.py:76
  152.3 18.5 %fusion.7 = f32[3,16,64,512]{3,2,0,1:T(8,128)} fusion(f32[3,16,64,512]{3,2,0,1:T(8,128)} %copy.84, f32[3,16,64,512]{3,2,1,0:T(8,128)} %get-tuple-element.12, f32[3,16,64,512]{3,2,1,0:T(8,128)} %get-tuple-element.11, f32[16,64,512]{2,1,0:T(8,128)} %get-tuple-element.19, f32[16,64,512]{2,1,0:T(8,128)} %get-tuple-element.20, ...), kind=kOutput, calls=%fused_computation.11 | convolution fusion | flops 9683075072 | bytes 34609152 | tf_op jit(solution)/shard_map/dot_general | solution.py:76
  170.9 6.7 %copy.96 = f32[3,16,64,512]{3,2,1,0:T(8,128)} copy(f32[3,16,64,512]{3,2,0,1:T(8,128)} %fusion.7) | data formatting | bytes 12582912 | tf_op jit(solution)/shard_map/add | solution.py:89
  (39 shorter events, 0.5 us)
Async XLA Ops:
  0.0 9.7 %copy-start.5 = (s32[256,1]{0,1:T(1,128)S(1)}, s32[256,1]{0,1:T(1,128)}, u32[]{:S(2)}) copy-start(s32[256,1]{0,1:T(1,128)} %param.12) | copy-start | bytes 3076
  0.0 9.9 %copy-start.7 = (s32[256]{0:T(256)S(1)}, s32[256]{0:T(256)}, u32[]{:S(2)}) copy-start(s32[256]{0:T(256)} %param.13) | copy-start | bytes 3076
  0.0 16.9 %copy-start.6 = (s32[256,4]{0,1:T(4,128)S(1)}, s32[256,4]{0,1:T(4,128)}, u32[]{:S(2)}) copy-start(s32[256,4]{0,1:T(4,128)} %param.11) | copy-start | bytes 12292
  2.5 1.3 copy-start.2
  4.0 13.5 %collective-permute-start.4 = (f32[3,32,512]{2,0,1:T(4,128)S(1)}, f32[3,32,512]{2,0,1:T(4,128)S(1)}, u32[]{:S(2)}, u32[]{:S(2)}) collective-permute-start(f32[3,32,512]{2,0,1:T(4,128)S(1)} %get-tuple-element.17), channel_id=1, source_target_pairs={{0,1},{1,2},{2,3},{3,4},{4,5},{5,6},{6,7},{7,8},{8,9},{9,10},{10,1... | collective-permute-start | bytes 589832 | tf_op jit(solution)/shard_map/ppermute | solution.py:20
  7.7 9.7 %collective-permute-start.5 = (f32[3,32,512]{2,0,1:T(4,128)S(1)}, f32[3,32,512]{2,0,1:T(4,128)S(1)}, u32[]{:S(2)}, u32[]{:S(2)}) collective-permute-start(f32[3,32,512]{2,0,1:T(4,128)S(1)} %get-tuple-element.18), channel_id=1, source_target_pairs={{1,0},{2,1},{3,2},{4,3},{5,4},{6,5},{7,6},{8,7},{9,8},{10,9},{11,1... | collective-permute-start | bytes 589832 | tf_op jit(solution)/shard_map/ppermute | solution.py:21
  10.7 33.8 %all-to-all-start = ((s32[32,1,16]{2,1,0:T(1,128)}), s32[32,1,16]{2,1,0:T(1,128)S(1)}, u32[]{:S(2)}, u32[]{:S(2)}) async-start(s32[32,1,16]{2,1,0:T(1,128)} %bitcast.8), calls=%async_computation | async-start | bytes 32768 | tf_op jit(solution)/shard_map/all_to_all | solution.py:62
  32.9 7.3 %copy-start.3 = (f32[3,256,512]{2,1,0:T(8,128)S(1)}, f32[3,256,512]{2,1,0:T(8,128)}, u32[]{:S(2)}) copy-start(f32[3,256,512]{2,1,0:T(8,128)} %param.9) | copy-start | bytes 4718596
  32.9 7.3 %copy-start.8 = (f32[256]{0:T(256)S(1)}, f32[256]{0:T(256)}, u32[]{:S(2)}) copy-start(f32[256]{0:T(256)} %param.10) | copy-start | bytes 3076
  44.5 13.9 %slice-start = ((s8[6291456]{0:T(1024)(128)(4,1)}), s8[2097152]{0:T(1024)(128)(4,1)S(1)}, s32[]{:S(2)}) async-start(s8[6291456]{0:T(1024)(128)(4,1)} %bitcast.56), calls=%async_computation.2 | async-start | bytes 4194304
  44.5 105.4 %all-to-all-start.1 = ((f32[32,16,1536]{2,1,0:T(8,128)}), f32[32,16,1536]{2,1,0:T(8,128)}, u32[]{:S(2)}, u32[]{:S(2)}) async-start(f32[32,16,1536]{2,1,0:T(8,128)} %fusion.39), calls=%async_computation.1 | async-start | bytes 6291456 | tf_op jit(solution)/shard_map/all_to_all | solution.py:55
  50.5 7.9 %slice-start.1 = ((s8[6291456]{0:T(1024)(128)(4,1)}), s8[4194304]{0:T(1024)(128)(4,1)S(1)}, s32[]{:S(2)}) async-start(s8[6291456]{0:T(1024)(128)(4,1)} %bitcast.56), calls=%async_computation.3 | async-start | bytes 8388608
  50.5 7.9 %copy-start = (f32[16,64,512]{2,1,0:T(8,128)S(1)}, f32[16,64,512]{2,1,0:T(8,128)}, u32[]{:S(2)}) copy-start(f32[16,64,512]{2,1,0:T(8,128)} %param.8) | copy-start | bytes 6291460
  53.0 70.5 %collective-permute-start = (f32[4,1,64,512]{3,2,1,0:T(8,128)}, f32[4,1,64,512]{3,2,1,0:T(8,128)S(1)}, u32[]{:S(2)}, u32[]{:S(2)}) collective-permute-start(f32[4,1,64,512]{3,2,1,0:T(8,128)} %get-tuple-element.13), channel_id=1, source_target_pairs={{8,0},{16,8},{24,16},{9,1},{17,9},{25,17},{10,2},{18,10},{26,18},{... | collective-permute-start | bytes 1572872 | tf_op jit(solution)/shard_map/ppermute | solution.py:21
  54.4 69.0 %collective-permute-start.1 = (f32[4,1,64,512]{3,2,1,0:T(8,128)}, f32[4,1,64,512]{3,2,1,0:T(8,128)S(1)}, u32[]{:S(2)}, u32[]{:S(2)}) collective-permute-start(f32[4,1,64,512]{3,2,1,0:T(8,128)} %get-tuple-element.14), channel_id=1, source_target_pairs={{0,8},{8,16},{16,24},{1,9},{9,17},{17,25},{2,10},{10,18},{18,26},{... | collective-permute-start | bytes 1572872 | tf_op jit(solution)/shard_map/ppermute | solution.py:20
  59.4 64.1 %collective-permute-start.2 = (f32[4,16,1,512]{3,2,1,0:T(1,128)}, f32[4,16,1,512]{3,2,1,0:T(1,128)S(1)}, u32[]{:S(2)}, u32[]{:S(2)}) collective-permute-start(f32[4,16,1,512]{3,2,1,0:T(1,128)} %get-tuple-element.15), channel_id=1, source_target_pairs={{1,0},{2,1},{3,2},{4,3},{5,4},{6,5},{7,6},{0,7},{9,8},{10,9},{11,1... | collective-permute-start | bytes 393224 | tf_op jit(solution)/shard_map/ppermute | solution.py:21
  60.3 63.1 %collective-permute-start.3 = (f32[4,16,1,512]{3,2,1,0:T(1,128)S(1)}, f32[4,16,1,512]{3,2,1,0:T(1,128)S(1)}, u32[]{:S(2)}, u32[]{:S(2)}) collective-permute-start(f32[4,16,1,512]{3,2,1,0:T(1,128)S(1)} %get-tuple-element.16), channel_id=1, source_target_pairs={{0,1},{1,2},{2,3},{3,4},{4,5},{5,6},{6,7},{7,0},{8,9},{9,10},{10,1... | collective-permute-start | bytes 393224 | tf_op jit(solution)/shard_map/ppermute | solution.py:20
  66.8 66.0 %copy-start.1 = (f32[16,64,512]{2,1,0:T(8,128)S(1)}, f32[16,64,512]{2,1,0:T(8,128)}, u32[]{:S(2)}) copy-start(f32[16,64,512]{2,1,0:T(8,128)} %param.8) | copy-start | bytes 6291460
  149.9 2.4 %copy-start.4 = (s32[16,64]{1,0:T(8,128)S(1)}, s32[16,64]{1,0:T(8,128)}, u32[]{:S(2)}) copy-start(s32[16,64]{1,0:T(8,128)} %multiply_add_fusion.1) | copy-start | bytes 12292
where the time goes:
time: 178 us
  waiting for transfers between devices  56.7 us (32%)
  other arithmetic  41.4 us (23%)
  local copies, waits for them, and re-layouts  32.1 us (18%)
  starting transfers between devices  25.3 us (14%)
  matrix products  21.7 us (12%)
    ppermute x3, waiting for transfers between devices, padded(): after = lax.ppermute(initial, axis, down)  56.7 us
    dot_general x1, matrix products, on_device(): deposit = jnp.dot(landing, got_tiles, precision=lax.Precision.HIGHEST)  18.5 us
    add x1, other arithmetic, on_device(): total + face_term(viscosity, azim_ext[3, :, 2:], velocity, azim_ext[:3, :...  17.2 us
    gather x1, local copies, waits for them, and re-layouts, on_device(): neighbours = jnp.take(extended, local_adj, axis=1)  13.3 us
    mul x1, other arithmetic, face_term(): return 0.5 * (mu + mu_other)[None] * (field_other - field)  9.29 us
    ppermute x3, starting transfers between devices, padded(): before = lax.ppermute(last, axis, up)  8.86 us
    unnamed x24, local copies, waits for them, and re-layouts  7.44 us
    reduce_sum x1, other arithmetic, on_device(): jnp.sum(neighbours - force[:, :, None, :], axis=2)  7.28 us
  transfers between devices with their start and end apart: 8, of which 1 were waited for; matrix products, arithmetic and copies ran while one was open for 36% of the time, Pallas kernels for 0%

commit v1 on v0

v1 whole, which is shorter than its diff:
```python
import functools

import jax
import jax.numpy as jnp
from jax import lax
from jax.experimental import pallas as pl
from jax.experimental.pallas import tpu as pltpu
from jax.sharding import PartitionSpec as P

HALO = 32
LANES = 128

step_size = 0.1
coupling = 0.2


def split(x):
    hi = x.astype(jnp.bfloat16)
    lo = (x - hi.astype(jnp.float32)).astype(jnp.bfloat16)
    return hi, lo


def dot(a, b):
    return jnp.dot(a, b, preferred_element_type=jnp.float32)


def exchange(n_ax, n_az, cap, vel, visc, force, rows, cols, base, got, gcell,
             velx, viscx, ext, send, scell, edges, edge_in, outbuf,
             load_sem, halo_send, halo_recv, tile_send, tile_recv,
             cell_send, cell_recv, own_sem, out_sem):
    n = n_ax * n_az
    ax, az = lax.axis_index("ax"), lax.axis_index("az")
    me = ax * n_az + az
    ncomp, na, nt, nr = vel.shape
    pan = force.shape[1]
    slots = n * cap

    def place(linear):
        return (linear // n_az, lax.rem(linear, n_az))

    def remote(src, dst, ssem, rsem, device):
        return pltpu.make_async_remote_copy(
            src_ref=src, dst_ref=dst, send_sem=ssem, recv_sem=rsem,
            device_id=device, device_id_type=pl.DeviceIdType.MESH)

    loads = [
        pltpu.make_async_copy(force, ext.at[:, pl.ds(HALO, pan)], load_sem.at[0]),
        pltpu.make_async_copy(vel, velx.at[:, pl.ds(1, na)], load_sem.at[1]),
        pltpu.make_async_copy(visc, viscx.at[pl.ds(1, na)], load_sem.at[2]),
    ]
    for c in loads:
        c.start()

    barrier = pltpu.get_barrier_semaphore()

    def greet(k, carry):
        pl.semaphore_signal(barrier, inc=1, device_id=place(lax.rem(me + k, n)),
                            device_id_type=pl.DeviceIdType.MESH)
        return carry

    lax.fori_loop(1, n, greet, 0)
    pl.semaphore_wait(barrier, n - 1)

    up, down = place(lax.rem(me + 1, n)), place(lax.rem(me + n - 1, n))
    ax_up, ax_down = lax.rem(ax + 1, n_ax), lax.rem(ax + n_ax - 1, n_ax)
    az_up, az_down = lax.rem(az + 1, n_az), lax.rem(az + n_az - 1, n_az)

    def halo(i, src, dst, device):
        return remote(src, dst, halo_send.at[i], halo_recv.at[i], device)

    fhalo = [
        halo(0, force.at[:, pl.ds(pan - HALO, HALO)], ext.at[:, pl.ds(0, HALO)], up),
        halo(1, force.at[:, pl.ds(0, HALO)], ext.at[:, pl.ds(HALO + pan, HALO)], down),
    ]
    for c in fhalo:
        c.start()
    ahalo = [
        halo(2, vel.at[:, na - 1], velx.at[:, 0], (ax_up, az)),
        halo(3, vel.at[:, 0], velx.at[:, na + 1], (ax_down, az)),
        halo(4, visc.at[na - 1], viscx.at[0], (ax_up, az)),
        halo(5, visc.at[0], viscx.at[na + 1], (ax_down, az)),
    ]

    dest_row, cell_col = rows[0:1, :], cols[:, 1:2]
    dest_col = cols[:, 0:1]
    same = dest_col == dest_row
    r0 = lax.broadcasted_iota(jnp.int32, (pan, pan), 0)
    r1 = lax.broadcasted_iota(jnp.int32, (pan, pan), 1)
    rank_row = jnp.sum((same & (r0 < r1)).astype(jnp.float32), axis=0, keepdims=True)
    rank_col = jnp.sum((same & (r1 < r0)).astype(jnp.float32), axis=1, keepdims=True)
    target = (dest_row * cap + rank_row).astype(jnp.int32)
    hits = lax.broadcasted_iota(jnp.int32, (slots, pan), 0) == target
    scale = jnp.sum(jnp.where(hits, coupling * rows[2:3, :], 0.0), axis=1, keepdims=True)
    q = lax.broadcasted_iota(jnp.int32, (pan, pan + 2 * HALO), 1).astype(jnp.float32)
    p = lax.broadcasted_iota(jnp.int32, (pan, pan + 2 * HALO), 0).astype(jnp.float32)
    count = (q == p + HALO).astype(jnp.float32)
    for k in range(4):
        count = count + (q == cols[:, 3 + k:4 + k]).astype(jnp.float32)
    pick = dot(hits.astype(jnp.float32).astype(jnp.bfloat16), count.astype(jnp.bfloat16))
    pick = pick.astype(jnp.bfloat16)

    big = jnp.floor((cell_col + 1.0) * (1.0 / 64.0))
    small = (cell_col + 1.0) - 64.0 * big
    lane = lax.broadcasted_iota(jnp.int32, (pan, LANES), 1).astype(jnp.float32)
    at_rank = lane == rank_col
    owner = (lax.broadcasted_iota(jnp.int32, (n, pan), 0).astype(jnp.float32) == dest_row)
    owner = owner.astype(jnp.float32).astype(jnp.bfloat16)
    cells = (64.0 * dot(owner, jnp.where(at_rank, big, 0.0).astype(jnp.bfloat16))
             + dot(owner, jnp.where(at_rank, small, 0.0).astype(jnp.bfloat16)) - 1.0)
    for d in range(n):
        scell[d] = cells[d:d + 1, :]

    loads[0].wait()
    for c in fhalo:
        c.wait()
    for c in range(ncomp):
        hi, lo = split(ext[c])
        tile = (dot(pick, hi) + dot(pick, lo)) * scale
        send[:, :, c * nr:(c + 1) * nr] = tile.reshape(n, cap, nr)

    def tiles_to(k):
        d = lax.rem(me + k, n)
        return (remote(send.at[d], got.at[me], tile_send.at[k], tile_recv.at[k], place(d)),
                remote(scell.at[d], gcell.at[me], cell_send.at[k], cell_recv.at[k], place(d)))

    for c in ahalo:
        c.start()
    loads[1].wait()
    loads[2].wait()
    for c in range(ncomp):
        edges[0, c] = velx[c, 1:na + 1, 0, :]
        edges[1, c] = velx[c, 1:na + 1, nt - 1, :]
    edges[0, ncomp] = viscx[1:na + 1, 0, :]
    edges[1, ncomp] = viscx[1:na + 1, nt - 1, :]
    zhalo = [
        halo(6, edges.at[1], edge_in.at[0], (ax, az_up)),
        halo(7, edges.at[0], edge_in.at[1], (ax, az_down)),
    ]
    for c in zhalo:
        c.start()

    def start_tiles(k, carry):
        a, b = tiles_to(k)
        a.start()
        b.start()
        return carry

    lax.fori_loop(1, n, start_tiles, 0)
    own = [pltpu.make_async_copy(send.at[me], got.at[me], own_sem.at[0]),
           pltpu.make_async_copy(scell.at[me], gcell.at[me], own_sem.at[1])]
    for c in own:
        c.start()

    for c in ahalo + zhalo:
        c.wait()

    @pl.when(ax == 0)
    def _():
        velx[:, 0] = jnp.zeros((ncomp, nt, nr), jnp.float32)
        viscx[0] = jnp.zeros((nt, nr), jnp.float32)

    @pl.when(ax == n_ax - 1)
    def _():
        velx[:, na + 1] = jnp.zeros((ncomp, nt, nr), jnp.float32)
        viscx[na + 1] = jnp.zeros((nt, nr), jnp.float32)

    row_id = lax.broadcasted_iota(jnp.int32, (nt, nr), 0)
    lane_id = lax.broadcasted_iota(jnp.int32, (nt, nr), 1)

    def neighbours(x, low, high):
        left = jnp.where(row_id == 0, low, pltpu.roll(x, 1, 0))
        right = jnp.where(row_id == nt - 1, high, pltpu.roll(x, nt - 1, 0))
        inner = jnp.where(lane_id == 0, 0.0, pltpu.roll(x, 1, 1))
        outer = jnp.where(lane_id == nr - 1, 0.0, pltpu.roll(x, nr - 1, 1))
        return left, right, inner, outer

    def stored(i, slot):
        return pltpu.make_async_copy(outbuf.at[slot], base.at[:, i], out_sem.at[slot])

    def plane(i, slot, first):
        if not first:
            stored(i - 2, slot).wait()
        mu = viscx[i + 1]
        sides = neighbours(mu, edge_in[0, ncomp, pl.ds(i, 1), :], edge_in[1, ncomp, pl.ds(i, 1), :])
        faces = [mu + s for s in (viscx[i], viscx[i + 2]) + sides]
        for c in range(ncomp):
            f = velx[c, i + 1]
            near = neighbours(f, edge_in[0, c, pl.ds(i, 1), :], edge_in[1, c, pl.ds(i, 1), :])
            near = (velx[c, i], velx[c, i + 2]) + near
            total = faces[0] * (near[0] - f)
            for w, g in zip(faces[1:], near[1:]):
                total = total + w * (g - f)
            outbuf[slot, c] = f + (0.5 * step_size) * total
        stored(i, slot).start()

    plane(0, 0, True)
    plane(1, 1, True)

    def planes(j, carry):
        plane(2 * j, 0, False)
        plane(2 * j + 1, 1, False)
        return carry

    lax.fori_loop(1, na // 2, planes, 0)
    stored(na - 2, 0).wait()
    stored(na - 1, 1).wait()

    for c in own:
        c.wait()

    def finish_tiles(k, carry):
        a, b = tiles_to(k)
        a.wait()
        b.wait()
        return carry

    lax.fori_loop(1, n, finish_tiles, 0)


def settle(cap, base, got, gcell, out, hi, lo, crow):
    step = pl.program_id(0)
    ncomp, blk, nt, nr = base.shape
    slots = got.shape[0]
    n = slots // cap

    @pl.when(step == 0)
    def _():
        cells = gcell[...].reshape(n, LANES)
        big = jnp.floor((cells + 1.0) * (1.0 / 64.0))
        small = (cells + 1.0) - 64.0 * big
        spread = (lax.broadcasted_iota(jnp.int32, (LANES, slots), 0)
                  == lax.rem(lax.broadcasted_iota(jnp.int32, (LANES, slots), 1), cap))
        spread = spread.astype(jnp.float32).astype(jnp.bfloat16)
        wide = 64.0 * dot(big.astype(jnp.bfloat16), spread) + dot(small.astype(jnp.bfloat16), spread)
        mine = (lax.broadcasted_iota(jnp.int32, (n, slots), 0)
                == lax.broadcasted_iota(jnp.int32, (n, slots), 1) // cap)
        crow[...] = jnp.sum(jnp.where(mine, wide, 0.0), axis=0, keepdims=True) - 1.0
        h, l = split(got[...])
        hi[...] = h
        lo[...] = l

    here = lax.broadcasted_iota(jnp.int32, (blk * nt, slots), 0) + step * (blk * nt)
    landing = (crow[...].astype(jnp.int32) == here).astype(jnp.float32).astype(jnp.bfloat16)
    for c in range(ncomp):
        cs = slice(c * nr, (c + 1) * nr)
        deposit = dot(landing, hi[:, cs]) + dot(landing, lo[:, cs])
        out[c] = base[c] + deposit.reshape(blk, nt, nr)


def on_device(n_ax, n_az, velocity, viscosity, force, area, adjacency, crossing, cell):
    n = n_ax * n_az
    ncomp, pan, nr = force.shape
    na, nt = velocity.shape[1:3]
    cap = max(2, 2 * pan // n)
    cap = -(-cap // 8) * 8
    f32 = jnp.float32
    first = lax.axis_index(("ax", "az")) * pan - HALO
    rows = jnp.concatenate([
        crossing.reshape(1, pan).astype(f32), cell.reshape(1, pan).astype(f32),
        area.reshape(1, pan), (adjacency - first).T.astype(f32), jnp.zeros((1, pan), f32)], axis=0)
    cols = rows.T
    any_ = pl.BlockSpec(memory_space=pl.ANY)
    vmem = pl.BlockSpec(memory_space=pltpu.VMEM)
    base, got, gcell = pl.pallas_call(
        functools.partial(exchange, n_ax, n_az, cap),
        out_shape=(jax.ShapeDtypeStruct(velocity.shape, f32),
                   jax.ShapeDtypeStruct((n, cap, ncomp * nr), f32),
                   jax.ShapeDtypeStruct((n, 1, LANES), f32)),
        in_specs=[any_, any_, any_, vmem, vmem],
        out_specs=(any_, any_, any_),
        scratch_shapes=[
            pltpu.VMEM((ncomp, na + 2, nt, nr), f32),
            pltpu.VMEM((na + 2, nt, nr), f32),
            pltpu.VMEM((ncomp, pan + 2 * HALO, nr), f32),
            pltpu.VMEM((n, cap, ncomp * nr), f32),
            pltpu.VMEM((n, 1, LANES), f32),
            pltpu.VMEM((2, ncomp + 1, na, nr), f32),
            pltpu.VMEM((2, ncomp + 1, na, nr), f32),
            pltpu.VMEM((2, ncomp, nt, nr), f32),
            pltpu.SemaphoreType.DMA((3,)),
            pltpu.SemaphoreType.DMA((8,)),
            pltpu.SemaphoreType.DMA((8,)),
            pltpu.SemaphoreType.DMA((n,)),
            pltpu.SemaphoreType.DMA((n,)),
            pltpu.SemaphoreType.DMA((n,)),
            pltpu.SemaphoreType.DMA((n,)),
            pltpu.SemaphoreType.DMA((2,)),
            pltpu.SemaphoreType.DMA((2,)),
        ],
        compiler_params=pltpu.CompilerParams(collective_id=0, has_side_effects=True),
        name="exchange",
    )(velocity, viscosity, force, rows, cols)
    slots = n * cap
    blk = max(1, 256 // nt)
    window = pl.BlockSpec((ncomp, blk, nt, nr), lambda s: (0, s, 0, 0))
    return pl.pallas_call(
        functools.partial(settle, cap),
        out_shape=jax.ShapeDtypeStruct(velocity.shape, f32),
        grid=(na // blk,),
        in_specs=[window,
                  pl.BlockSpec((slots, ncomp * nr), lambda s: (0, 0)),
                  pl.BlockSpec((n, 1, LANES), lambda s: (0, 0, 0))],
        out_specs=window,
        scratch_shapes=[pltpu.VMEM((slots, ncomp * nr), jnp.bfloat16),
                        pltpu.VMEM((slots, ncomp * nr), jnp.bfloat16),
                        pltpu.VMEM((1, slots), f32)],
        name="settle",
    )(base, got.reshape(slots, ncomp * nr), gcell)


def solution(mesh):
    n_ax, n_az = mesh.shape["ax"], mesh.shape["az"]
    in_specs = (
        P(None, "ax", "az", None),
        P("ax", "az", None),
        P(None, ("ax", "az"), None),
        P(("ax", "az")),
        P(("ax", "az"), None),
        P(("ax", "az"), None),
        P(("ax", "az")),
    )
    return jax.shard_map(
        functools.partial(on_device, n_ax, n_az), mesh=mesh, in_specs=in_specs,
        out_specs=P(None, "ax", "az", None), check_vma=False)
```

time: 178 us -> 104 us (0.58)
  the two profiles are of different devices: /device:TPU:9 before, /device:TPU:25 now
where the time goes in v1:
time: 104 us; the launch traced here: 103 us
  Pallas kernels  99.8 us (96%)
  other arithmetic  2.05 us (2%)
  local copies, waits for them, and re-layouts  1.49 us (1%)
    pallas_call x1, Pallas kernels, on_device(): pl.pallas_call(functools.partial(exchange, n_ax, n_az, cap), out_shape=(j...  90.2 us
    pallas_call x1, Pallas kernels, on_device(): pl.pallas_call(functools.partial(settle, cap), out_shape=jax.ShapeDtypeSt...  9.62 us

profile of v1, /device:TPU:25, one launch (start us, length us, event | category | flops | bytes accessed | tf_op | source)
XLA Modules:
  0.0 103.3 jit_solution(1372906774749978489)
XLA Ops:
  0.0 0.7 convert_bitcast_fusion.1
  0.7 0.7 convert_element_type.28
  1.4 0.7 convert_bitcast_fusion
  2.1 0.7 concatenate.3.rows
  2.8 0.0 copy-start
  2.8 0.8 copy.17
  3.6 0.0 copy-done
  3.6 90.2 %exchange.1 = (f32[3,16,64,512]{3,2,1,0:T(8,128)}, f32[32,16,1536]{2,1,0:T(8,128)}, f32[32,1,128]{2,1,0:T(1,128)}) custom-call(f32[3,16,64,512]{3,2,1,0:T(8,128)} %vel.1, f32[16,64,512]{2,1,0:T(8,128)} %visc.1, f32[3,256,512]{2,1,0:T(8,128)} %force.1, f32[8,256]{1,0:T(8,128)} %copy-done, f32[256,8]{1,0:T(8,128)} %bitcast.9), custom_call_target="tpu_custom_call" | custom-call | tf_op jit(solution)/shard_map/exchange/pallas_call | solution.py:264
  93.7 9.6 %settle.1 = f32[3,16,64,512]{3,2,1,0:T(8,128)} custom-call(f32[3,16,64,512]{3,2,1,0:T(8,128)} %get-tuple-element.8.base, f32[512,1536]{1,0:T(8,128)} %bitcast.8, f32[32,1,128]{2,1,0:T(1,128)} %get-tuple-element.10.gcell), custom_call_target="tpu_custom_call" | custom-call | tf_op jit(solution)/shard_map/settle/pallas_call | solution.py:296
  (1 shorter events, 0.0 us)
Async XLA Ops:
  2.8 0.8 copy-start

commit v2 on v1

v2 whole, which is shorter than its diff:
```python
import functools

import jax
import jax.numpy as jnp
from jax import lax
from jax.experimental import pallas as pl
from jax.experimental.pallas import tpu as pltpu
from jax.sharding import PartitionSpec as P

HALO = 32
LANES = 128

step_size = 0.1
coupling = 0.2


def split(x):
    hi = x.astype(jnp.bfloat16)
    lo = (x - hi.astype(jnp.float32)).astype(jnp.bfloat16)
    return hi, lo


def dot(a, b):
    return jnp.dot(a, b, preferred_element_type=jnp.float32)


def wide_row(cells, cap):
    m = cells.shape[0]
    slots = m * cap
    big = jnp.floor((cells + 1.0) * (1.0 / 64.0))
    small = (cells + 1.0) - 64.0 * big
    spread = (lax.broadcasted_iota(jnp.int32, (LANES, slots), 0)
              == lax.rem(lax.broadcasted_iota(jnp.int32, (LANES, slots), 1), cap))
    spread = spread.astype(jnp.float32).astype(jnp.bfloat16)
    wide = 64.0 * dot(big.astype(jnp.bfloat16), spread) + dot(small.astype(jnp.bfloat16), spread)
    mine = (lax.broadcasted_iota(jnp.int32, (m, slots), 0)
            == lax.broadcasted_iota(jnp.int32, (m, slots), 1) // cap)
    return jnp.sum(jnp.where(mine, wide, 0.0), axis=0, keepdims=True) - 1.0


def landing_of(crow, first, count):
    here = lax.broadcasted_iota(jnp.int32, (count, crow.shape[1]), 0) + first
    return (crow.astype(jnp.int32) == here).astype(jnp.float32).astype(jnp.bfloat16)


def exchange(n_ax, n_az, cap, vel, visc, force, dest_i, cell_i, area, adj_i, base, got, gcell,
             velx, viscx, ext, exthi, extlo, send, scell, edges, edge_in, acc,
             tiles, tcell, thi, tlo,
             load_sem, halo_send, halo_recv, tile_send, tile_recv,
             cell_send, cell_recv, own_sem, out_sem):
    n, half_n = n_ax * n_az, n_az // 2
    early = n_ax // 2
    ax, az = lax.axis_index("ax"), lax.axis_index("az")
    me = ax * n_az + az
    half, spot = az // half_n, lax.rem(az, half_n)
    ncomp, na, nt, nr = vel.shape
    pan = force.shape[1]
    slots = n * cap
    f32, bf16 = jnp.float32, jnp.bfloat16

    def place(linear):
        return (linear // n_az, lax.rem(linear, n_az))

    def remote(src, dst, ssem, rsem, device):
        return pltpu.make_async_remote_copy(
            src_ref=src, dst_ref=dst, send_sem=ssem, recv_sem=rsem,
            device_id=device, device_id_type=pl.DeviceIdType.MESH)

    barrier = pltpu.get_barrier_semaphore()

    def greet(k, carry):
        pl.semaphore_signal(barrier, inc=1, device_id=place(lax.rem(me + k, n)),
                            device_id_type=pl.DeviceIdType.MESH)
        return carry

    lax.fori_loop(1, n, greet, 0)
    loads = [
        pltpu.make_async_copy(force, ext.at[:, pl.ds(HALO, pan)], load_sem.at[0]),
        pltpu.make_async_copy(vel, velx.at[:, pl.ds(1, na)], load_sem.at[1]),
        pltpu.make_async_copy(visc, viscx.at[pl.ds(1, na)], load_sem.at[2]),
    ]
    for c in loads:
        c.start()

    dest_row, cell_row = dest_i[...].astype(f32), cell_i[...].astype(f32)
    adj = (adj_i[...] - (me * pan - HALO)).astype(f32)
    rows = jnp.concatenate([dest_row, cell_row, adj, dest_row, dest_row], axis=0)
    cols = rows.T
    dest_col, cell_col = cols[:, 0:1], cols[:, 1:2]
    same = dest_col == dest_row
    r0 = lax.broadcasted_iota(jnp.int32, (pan, pan), 0)
    r1 = lax.broadcasted_iota(jnp.int32, (pan, pan), 1)
    rank_row = jnp.sum((same & (r0 < r1)).astype(f32), axis=0, keepdims=True)
    rank_col = jnp.sum((same & (r1 < r0)).astype(f32), axis=1, keepdims=True)
    dax = jnp.floor(dest_row * (1.0 / n_az))
    daz = dest_row - n_az * dax
    dhalf = jnp.floor(daz * (1.0 / half_n))
    turn = dax - ax.astype(f32)
    turn = jnp.where(turn < 0.0, turn + n_ax, turn)
    group = turn + jnp.where(dhalf == half.astype(f32), float(n_ax), 0.0)
    peer = group * half_n + (daz - half_n * dhalf)
    target = (peer * cap + rank_row).astype(jnp.int32)
    hits = lax.broadcasted_iota(jnp.int32, (slots, pan), 0) == target
    scale = jnp.sum(jnp.where(hits, coupling * area[...], 0.0), axis=1, keepdims=True)
    q = lax.broadcasted_iota(jnp.int32, (pan, pan + 2 * HALO), 1).astype(f32)
    p = lax.broadcasted_iota(jnp.int32, (pan, pan + 2 * HALO), 0).astype(f32)
    count = (q == p + HALO).astype(f32)
    for k in range(4):
        count = count + (q == cols[:, 2 + k:3 + k]).astype(f32)
    pick = dot(hits.astype(f32).astype(bf16), count.astype(bf16)).astype(bf16)

    pl.semaphore_wait(barrier, n - 1)

    up, down = place(lax.rem(me + 1, n)), place(lax.rem(me + n - 1, n))
    ax_up, ax_down = lax.rem(ax + 1, n_ax), lax.rem(ax + n_ax - 1, n_ax)
    az_up, az_down = lax.rem(az + 1, n_az), lax.rem(az + n_az - 1, n_az)

    def halo(i, src, dst, device):
        return remote(src, dst, halo_send.at[i], halo_recv.at[i], device)

    fhalo = [
        halo(0, force.at[:, pl.ds(pan - HALO, HALO)], ext.at[:, pl.ds(0, HALO)], up),
        halo(1, force.at[:, pl.ds(0, HALO)], ext.at[:, pl.ds(HALO + pan, HALO)], down),
    ]
    ahalo = [
        halo(2, vel.at[:, na - 1], velx.at[:, 0], (ax_up, az)),
        halo(3, vel.at[:, 0], velx.at[:, na + 1], (ax_down, az)),
        halo(4, visc.at[na - 1], viscx.at[0], (ax_up, az)),
        halo(5, visc.at[0], viscx.at[na + 1], (ax_down, az)),
    ]
    for c in fhalo:
        c.start()

    big = jnp.floor((cell_col + 1.0) * (1.0 / 64.0))
    small = (cell_col + 1.0) - 64.0 * big
    at_rank = lax.broadcasted_iota(jnp.int32, (pan, LANES), 1).astype(f32) == rank_col
    owner = lax.broadcasted_iota(jnp.int32, (n, pan), 0).astype(f32) == peer
    owner = owner.astype(f32).astype(bf16)
    cells = (64.0 * dot(owner, jnp.where(at_rank, big, 0.0).astype(bf16))
             + dot(owner, jnp.where(at_rank, small, 0.0).astype(bf16)) - 1.0)
    for d in range(n):
        scell[d] = cells[d:d + 1, :]

    def split_force(lo_row, hi_row):
        h, l = split(ext[:, lo_row:hi_row])
        exthi[:, lo_row:hi_row] = h
        extlo[:, lo_row:hi_row] = l

    loads[0].wait()
    split_force(HALO, HALO + pan)
    for c in fhalo:
        c.wait()
    split_force(0, HALO)
    split_force(HALO + pan, pan + 2 * HALO)

    def tiles_to(g, i):
        there = lax.rem(spot + i, half_n)
        side = 1 - half if g < n_ax else half
        device = (lax.rem(ax + g % n_ax, n_ax), side * half_n + there)
        src, k = g * half_n + there, g * half_n + i
        if early <= g < n_ax:
            at = (g - early) * half_n + spot
            tile_at, cell_at = got.at[at], gcell.at[at]
        else:
            at = (g if g < early else g - n_ax + early) * half_n + spot
            tile_at, cell_at = tiles.at[at], tcell.at[at]
        return (remote(send.at[src], tile_at, tile_send.at[k], tile_recv.at[k], device),
                remote(scell.at[src], cell_at, cell_send.at[k], cell_recv.at[k], device))

    def each_tile(groups, act):
        for g in groups:
            def body(i, carry):
                for c in tiles_to(g, i):
                    act(c)
                return carry
            lax.fori_loop(1 if g == n_ax else 0, half_n, body, 0)

    for part in range(2):
        r = slice(part * (slots // 2), (part + 1) * (slots // 2))
        for c in range(ncomp):
            tile = (dot(pick[r], exthi[c]) + dot(pick[r], extlo[c])) * scale[r]
            send[part * (n // 2):(part + 1) * (n // 2), :, c * nr:(c + 1) * nr] = (
                tile.reshape(n // 2, cap, nr))
        each_tile(range(part * n_ax, (part + 1) * n_ax), lambda c: c.start())
        if part == 0:
            for c in ahalo:
                c.start()
    own_src, own_dst = n_ax * half_n + spot, early * half_n + spot
    own = [pltpu.make_async_copy(send.at[own_src], tiles.at[own_dst], own_sem.at[0]),
           pltpu.make_async_copy(scell.at[own_src], tcell.at[own_dst], own_sem.at[1])]
    for c in own:
        c.start()

    loads[1].wait()
    loads[2].wait()
    for c in range(ncomp):
        edges[0, c] = velx[c, 1:na + 1, 0, :]
        edges[1, c] = velx[c, 1:na + 1, nt - 1, :]
    edges[0, ncomp] = viscx[1:na + 1, 0, :]
    edges[1, ncomp] = viscx[1:na + 1, nt - 1, :]
    zhalo = [
        halo(6, edges.at[1], edge_in.at[0], (ax, az_up)),
        halo(7, edges.at[0], edge_in.at[1], (ax, az_down)),
    ]
    for c in zhalo:
        c.start()
    for c in ahalo + zhalo:
        c.wait()

    @pl.when(ax == 0)
    def _():
        velx[:, 0] = jnp.zeros((ncomp, nt, nr), f32)
        viscx[0] = jnp.zeros((nt, nr), f32)

    @pl.when(ax == n_ax - 1)
    def _():
        velx[:, na + 1] = jnp.zeros((ncomp, nt, nr), f32)
        viscx[na + 1] = jnp.zeros((nt, nr), f32)

    row_id = lax.broadcasted_iota(jnp.int32, (nt, nr), 0)
    lane_id = lax.broadcasted_iota(jnp.int32, (nt, nr), 1)

    def neighbours(x, low, high):
        left = jnp.where(row_id == 0, low, pltpu.roll(x, 1, 0))
        right = jnp.where(row_id == nt - 1, high, pltpu.roll(x, nt - 1, 0))
        inner = jnp.where(lane_id == 0, 0.0, pltpu.roll(x, 1, 1))
        outer = jnp.where(lane_id == nr - 1, 0.0, pltpu.roll(x, nr - 1, 1))
        return left, right, inner, outer

    def plane(i, carry):
        mu = viscx[i + 1]
        sides = neighbours(mu, edge_in[0, ncomp, pl.ds(i, 1), :], edge_in[1, ncomp, pl.ds(i, 1), :])
        faces = [mu + s for s in (viscx[i], viscx[i + 2]) + sides]
        for c in range(ncomp):
            f = velx[c, i + 1]
            near = neighbours(f, edge_in[0, c, pl.ds(i, 1), :], edge_in[1, c, pl.ds(i, 1), :])
            near = (velx[c, i], velx[c, i + 2]) + near
            total = faces[0] * (near[0] - f)
            for w, g in zip(faces[1:], near[1:]):
                total = total + w * (g - f)
            acc[c, i] = f + (0.5 * step_size) * total
        return carry

    lax.fori_loop(0, na, plane, 0)

    late = list(range(early, n_ax))
    for c in own:
        c.wait()
    each_tile([g for g in range(2 * n_ax) if g not in late], lambda c: c.wait())
    h, l = split(tiles[...].reshape(-1, ncomp * nr))
    thi[...] = h
    tlo[...] = l
    crow = wide_row(tcell[...].reshape(-1, LANES), cap)
    blk = max(1, 256 // nt)

    def stored(j):
        return pltpu.make_async_copy(acc.at[:, pl.ds(j * blk, blk)],
                                     base.at[:, pl.ds(j * blk, blk)], out_sem.at[j])

    for j in range(na // blk):
        landing = landing_of(crow, j * blk * nt, blk * nt)
        for c in range(ncomp):
            cs = slice(c * nr, (c + 1) * nr)
            deposit = dot(landing, thi[:, cs]) + dot(landing, tlo[:, cs])
            acc[c, j * blk:(j + 1) * blk] += deposit.reshape(blk, nt, nr)
        stored(j).start()
    for j in range(na // blk):
        stored(j).wait()
    each_tile(late, lambda c: c.wait())


def settle(cap, base, got, gcell, out, hi, lo, crow):
    step = pl.program_id(0)
    ncomp, blk, nt, nr = base.shape

    @pl.when(step == 0)
    def _():
        crow[...] = wide_row(gcell[...].reshape(-1, LANES), cap)
        h, l = split(got[...])
        hi[...] = h
        lo[...] = l

    landing = landing_of(crow[...], step * (blk * nt), blk * nt)
    for c in range(ncomp):
        cs = slice(c * nr, (c + 1) * nr)
        deposit = dot(landing, hi[:, cs]) + dot(landing, lo[:, cs])
        out[c] = base[c] + deposit.reshape(blk, nt, nr)


def on_device(n_ax, n_az, velocity, viscosity, force, area, adjacency, crossing, cell):
    n, half_n = n_ax * n_az, n_az // 2
    ncomp, pan, nr = force.shape
    na, nt = velocity.shape[1:3]
    cap = max(2, 2 * pan // n)
    cap = -(-cap // 8) * 8
    slots = n * cap
    late = (n_ax - n_ax // 2) * half_n
    soon = n - late
    f32, bf16 = jnp.float32, jnp.bfloat16
    any_ = pl.BlockSpec(memory_space=pl.ANY)
    vmem = pl.BlockSpec(memory_space=pltpu.VMEM)
    dma = pltpu.SemaphoreType.DMA
    base, got, gcell = pl.pallas_call(
        functools.partial(exchange, n_ax, n_az, cap),
        out_shape=(jax.ShapeDtypeStruct(velocity.shape, f32),
                   jax.ShapeDtypeStruct((late, cap, ncomp * nr), f32),
                   jax.ShapeDtypeStruct((late, 1, LANES), f32)),
        in_specs=[any_, any_, any_, vmem, vmem, vmem, vmem],
        out_specs=(any_, any_, any_),
        scratch_shapes=[
            pltpu.VMEM((ncomp, na + 2, nt, nr), f32),
            pltpu.VMEM((na + 2, nt, nr), f32),
            pltpu.VMEM((ncomp, pan + 2 * HALO, nr), f32),
            pltpu.VMEM((ncomp, pan + 2 * HALO, nr), bf16),
            pltpu.VMEM((ncomp, pan + 2 * HALO, nr), bf16),
            pltpu.VMEM((n, cap, ncomp * nr), f32),
            pltpu.VMEM((n, 1, LANES), f32),
            pltpu.VMEM((2, ncomp + 1, na, nr), f32),
            pltpu.VMEM((2, ncomp + 1, na, nr), f32),
            pltpu.VMEM((ncomp, na, nt, nr), f32),
            pltpu.VMEM((soon, cap, ncomp * nr), f32),
            pltpu.VMEM((soon, 1, LANES), f32),
            pltpu.VMEM((soon * cap, ncomp * nr), bf16),
            pltpu.VMEM((soon * cap, ncomp * nr), bf16),
            dma((3,)), dma((8,)), dma((8,)), dma((n,)), dma((n,)), dma((n,)), dma((n,)),
            dma((2,)), dma((na,)),
        ],
        compiler_params=pltpu.CompilerParams(collective_id=0, has_side_effects=True),
        name="exchange",
    )(velocity, viscosity, force, crossing.reshape(1, pan), cell.reshape(1, pan),
      area.reshape(1, pan), adjacency.T)
    blk = max(1, 128 // nt)
    window = pl.BlockSpec((ncomp, blk, nt, nr), lambda s: (0, s, 0, 0))
    return pl.pallas_call(
        functools.partial(settle, cap),
        out_shape=jax.ShapeDtypeStruct(velocity.shape, f32),
        grid=(na // blk,),
        in_specs=[window,
                  pl.BlockSpec((late * cap, ncomp * nr), lambda s: (0, 0)),
                  pl.BlockSpec((late, 1, LANES), lambda s: (0, 0, 0))],
        out_specs=window,
        scratch_shapes=[pltpu.VMEM((late * cap, ncomp * nr), bf16),
                        pltpu.VMEM((late * cap, ncomp * nr), bf16),
                        pltpu.VMEM((1, late * cap), f32)],
        name="settle",
    )(base, got.reshape(late * cap, ncomp * nr), gcell)


def solution(mesh):
    n_ax, n_az = mesh.shape["ax"], mesh.shape["az"]
    in_specs = (
        P(None, "ax", "az", None),
        P("ax", "az", None),
        P(None, ("ax", "az"), None),
        P(("ax", "az")),
        P(("ax", "az"), None),
        P(("ax", "az"), None),
        P(("ax", "az")),
    )
    return jax.shard_map(
        functools.partial(on_device, n_ax, n_az), mesh=mesh, in_specs=in_specs,
        out_specs=P(None, "ax", "az", None), check_vma=False)
```

time: 104 us -> 109 us (1.048)
  the two profiles are of different devices: /device:TPU:25 before, /device:TPU:9 now
where the time goes in v2:
time: 109 us
  Pallas kernels  109 us (100%)
    pallas_call x1, Pallas kernels, on_device(): pl.pallas_call(functools.partial(exchange, n_ax, n_az, cap), out_shape=(j...  99.7 us
    pallas_call x1, Pallas kernels, on_device(): pl.pallas_call(functools.partial(settle, cap), out_shape=jax.ShapeDtypeSt...  9.44 us

profile of v2, /device:TPU:9, one launch (start us, length us, event | category | flops | bytes accessed | tf_op | source)
XLA Modules:
  0.0 109.2 jit_solution(16615302256131900539)
XLA Ops:
  0.0 99.7 %exchange.1 = (f32[3,16,64,512]{3,2,1,0:T(8,128)}, f32[8,16,1536]{2,1,0:T(8,128)}, f32[8,1,128]{2,1,0:T(1,128)}) custom-call(f32[3,16,64,512]{3,2,1,0:T(8,128)} %vel.1, f32[16,64,512]{2,1,0:T(8,128)} %visc.1, f32[3,256,512]{2,1,0:T(8,128)} %force.1, s32[1,256]{1,0:T(1,128)} %bitcast.7, s32[1,256]{1,0:T(1,128)} %bitcast.8, f32[1,256]{1,0:T(1,128)} %bitcast.9, ...), custom_call_target="tpu_custom_call" | custom-call | tf_op jit(solution)/shard_map/exchange/pallas_call | solution.py:303
  99.7 9.4 %settle.1 = f32[3,16,64,512]{3,2,1,0:T(8,128)} custom-call(f32[3,16,64,512]{3,2,1,0:T(8,128)} %get-tuple-element.8.base, f32[128,1536]{1,0:T(8,128)} %bitcast.5, f32[8,1,128]{2,1,0:T(1,128)} %get-tuple-element.10.gcell), custom_call_target="tpu_custom_call" | custom-call | tf_op jit(solution)/shard_map/settle/pallas_call | solution.py:334

commit v3 on v2

--- a/solution.py
+++ b/solution.py
@@ -109,6 +109,14 @@
         count = count + (q == cols[:, 2 + k:3 + k]).astype(f32)
     pick = dot(hits.astype(f32).astype(bf16), count.astype(bf16)).astype(bf16)
 
+    loads[1].wait()
+    loads[2].wait()
+    for c in range(ncomp):
+        edges[0, c] = velx[c, 1:na + 1, 0, :]
+        edges[1, c] = velx[c, 1:na + 1, nt - 1, :]
+    edges[0, ncomp] = viscx[1:na + 1, 0, :]
+    edges[1, ncomp] = viscx[1:na + 1, nt - 1, :]
+
     pl.semaphore_wait(barrier, n - 1)
 
     up, down = place(lax.rem(me + 1, n)), place(lax.rem(me + n - 1, n))
@@ -128,7 +136,11 @@
         halo(4, visc.at[na - 1], viscx.at[0], (ax_up, az)),
         halo(5, visc.at[0], viscx.at[na + 1], (ax_down, az)),
     ]
-    for c in fhalo:
+    zhalo = [
+        halo(6, edges.at[1], edge_in.at[0], (ax, az_up)),
+        halo(7, edges.at[0], edge_in.at[1], (ax, az_down)),
+    ]
+    for c in fhalo + zhalo + ahalo:
         c.start()
 
     big = jnp.floor((cell_col + 1.0) * (1.0 / 64.0))
@@ -182,28 +194,12 @@
             send[part * (n // 2):(part + 1) * (n // 2), :, c * nr:(c + 1) * nr] = (
                 tile.reshape(n // 2, cap, nr))
         each_tile(range(part * n_ax, (part + 1) * n_ax), lambda c: c.start())
-        if part == 0:
-            for c in ahalo:
-                c.start()
     own_src, own_dst = n_ax * half_n + spot, early * half_n + spot
     own = [pltpu.make_async_copy(send.at[own_src], tiles.at[own_dst], own_sem.at[0]),
            pltpu.make_async_copy(scell.at[own_src], tcell.at[own_dst], own_sem.at[1])]
     for c in own:
         c.start()
 
-    loads[1].wait()
-    loads[2].wait()
-    for c in range(ncomp):
-        edges[0, c] = velx[c, 1:na + 1, 0, :]
-        edges[1, c] = velx[c, 1:na + 1, nt - 1, :]
-    edges[0, ncomp] = viscx[1:na + 1, 0, :]
-    edges[1, ncomp] = viscx[1:na + 1, nt - 1, :]
-    zhalo = [
-        halo(6, edges.at[1], edge_in.at[0], (ax, az_up)),
-        halo(7, edges.at[0], edge_in.at[1], (ax, az_down)),
-    ]
-    for c in zhalo:
-        c.start()
     for c in ahalo + zhalo:
         c.wait()
 
@@ -298,14 +294,17 @@
     soon = n - late
     f32, bf16 = jnp.float32, jnp.bfloat16
     any_ = pl.BlockSpec(memory_space=pl.ANY)
+    hbm = pl.BlockSpec(memory_space=pltpu.HBM)
     vmem = pl.BlockSpec(memory_space=pltpu.VMEM)
     dma = pltpu.SemaphoreType.DMA
+    velocity, viscosity, force = (
+        pltpu.with_memory_space_constraint(x, pltpu.HBM) for x in (velocity, viscosity, force))
     base, got, gcell = pl.pallas_call(
         functools.partial(exchange, n_ax, n_az, cap),
         out_shape=(jax.ShapeDtypeStruct(velocity.shape, f32),
                    jax.ShapeDtypeStruct((late, cap, ncomp * nr), f32),
                    jax.ShapeDtypeStruct((late, 1, LANES), f32)),
-        in_specs=[any_, any_, any_, vmem, vmem, vmem, vmem],
+        in_specs=[hbm, hbm, hbm, vmem, vmem, vmem, vmem],
         out_specs=(any_, any_, any_),
         scratch_shapes=[
             pltpu.VMEM((ncomp, na + 2, nt, nr), f32),
@@ -325,7 +324,8 @@
             dma((3,)), dma((8,)), dma((8,)), dma((n,)), dma((n,)), dma((n,)), dma((n,)),
             dma((2,)), dma((na,)),
         ],
-        compiler_params=pltpu.CompilerParams(collective_id=0, has_side_effects=True),
+        compiler_params=pltpu.CompilerParams(collective_id=0, has_side_effects=True,
+                                             vmem_limit_bytes=40 << 20),
         name="exchange",
     )(velocity, viscosity, force, crossing.reshape(1, pan), cell.reshape(1, pan),
       area.reshape(1, pan), adjacency.T)
@@ -342,6 +342,7 @@
         scratch_shapes=[pltpu.VMEM((late * cap, ncomp * nr), bf16),
                         pltpu.VMEM((late * cap, ncomp * nr), bf16),
                         pltpu.VMEM((1, late * cap), f32)],
+        compiler_params=pltpu.CompilerParams(vmem_limit_bytes=16 << 20),
         name="settle",
     )(base, got.reshape(late * cap, ncomp * nr), gcell)
 

time: 109 us -> 100 us (0.917)
  the two profiles are of different devices: /device:TPU:9 before, /device:TPU:0 now
where the time goes in v3:
time: 100 us; the launch traced here: 99.9 us
  Pallas kernels  97.1 us (97%)
  local copies, waits for them, and re-layouts  2.72 us (3%)
    pallas_call x1, Pallas kernels, on_device(): pl.pallas_call(functools.partial(exchange, n_ax, n_az, cap), out_shape=(j...  91.3 us
    pallas_call x1, Pallas kernels, on_device(): pl.pallas_call(functools.partial(settle, cap), out_shape=jax.ShapeDtypeSt...  5.83 us
    unnamed x8, local copies, waits for them, and re-layouts  2.72 us

profile of v3, /device:TPU:0, one launch (start us, length us, event | category | flops | bytes accessed | tf_op | source)
XLA Modules:
  0.0 99.9 jit_solution(1960413105764423519)
XLA Ops:
  0.0 0.0 copy-start
  0.0 0.7 copy-done
  0.7 0.0 copy-start.1
  0.7 0.7 copy-done.1
  1.4 0.0 copy-start.2
  1.4 0.7 copy-done.2
  2.0 0.0 copy-start.3
  2.0 0.7 copy-done.3
  2.7 91.3 %exchange.1 = (f32[3,16,64,512]{3,2,1,0:T(8,128)S(1)}, f32[8,16,1536]{2,1,0:T(8,128)S(1)}, f32[8,1,128]{2,1,0:T(1,128)S(1)}) custom-call(f32[3,16,64,512]{3,2,1,0:T(8,128)} %vel.1, f32[16,64,512]{2,1,0:T(8,128)} %visc.1, f32[3,256,512]{2,1,0:T(8,128)} %force.1, s32[1,256]{1,0:T(1,128)S(1)} %bitcast.7, s32[1,256]{1,0:T(1,128)S(1)} %bitcast.8, ...), custom_call_target="tpu_custom_call" | custom-call | tf_op jit(solution)/shard_map/exchange/pallas_call | solution.py:302
  94.0 5.8 %settle.1 = f32[3,16,64,512]{3,2,1,0:T(8,128)} custom-call(f32[3,16,64,512]{3,2,1,0:T(8,128)S(1)} %get-tuple-element.8.base, f32[128,1536]{1,0:T(8,128)S(1)} %bitcast.5, f32[8,1,128]{2,1,0:T(1,128)S(1)} %get-tuple-element.10.gcell), custom_call_target="tpu_custom_call" | custom-call | tf_op jit(solution)/shard_map/settle/pallas_call | solution.py:334
Async XLA Ops:
  0.0 0.7 copy-start
  0.7 0.7 copy-start.1
  1.4 0.7 copy-start.2
  2.0 0.7 copy-start.3
